TPU v7x, 512 devices: a whole 4x4x16 slice. The times are simulated.
512 devices in a mesh: row: 16 (over z_lo, y), col: 32 (over z_hi, x, core).
Axes of the slice: x: 4, y: 4, z: 16 (z_hi: 4, z_lo: 4; z = z_hi * 4 + z_lo), core: 2. Of those that a mesh axis runs over, the one named last changes fastest.
Arguments:
- ancestor: float32 [20480, 20480], P('row', 'col'), as said below
- factor_rows: float32 [2, 256, 20480], P(None, 'row', 'col'), may hold values from -6 to 6
- block_lists: int32 [2, 8], replicated, may hold values from 0 to 15, as said below
Outputs:
- inverse_panel: float32 [2, 20480, 256], P(None, ('row', 'col'))
- inverse_rows: float32 [2, 256, 20480], P(None, 'col', 'row')
Inputs may be any that keep to these rules, and one draw needn't show every extreme that they name: `block_lists`: each row lists 8 distinct blocks in increasing order; the first block 0 and the last block 15 are in every row. ancestor is symmetric: ancestor[i, j] = ancestor[j, i].
All inputs are finite; a program needn't handle non-finite values.
Results may differ from a plain program's by a relative error of at most 0.000071.
Values sent between devices are 32-bit elements; how exact they have to be, the bound alone decides.
A program may use at most 64 MiB of HBM per device.

v0:
```python
import jax
import jax.numpy as jnp
from jax import lax
from jax.sharding import PartitionSpec as P

BS = 1280


def listed_mask(block_lists, blocks):
    return jnp.any(block_lists[:, :, None] == blocks[None, None, :], axis=1).astype(jnp.float32)


def per_device(ancestor, factor_rows, block_lists):
    local_rows = ancestor.shape[0]
    local_cols = ancestor.shape[1]
    col_count = lax.axis_size("col")
    row_place = lax.axis_index("row")
    col_place = lax.axis_index("col")
    col_blocks = (col_place * local_cols + lax.iota(jnp.int32, local_cols)) // BS
    masked = factor_rows * listed_mask(block_lists, col_blocks)[:, None, :]
    gathered = lax.all_gather(masked, "row", axis=1, tiled=True)
    rows_out = local_rows // col_count
    summed = lax.psum_scatter(
        -jnp.einsum(
            "ic,swc->isw",
            ancestor,
            gathered,
            precision=lax.Precision.HIGHEST,
            preferred_element_type=jnp.float32,
        ),
        "col",
        scatter_dimension=0,
        tiled=True,
    )
    first_row = (row_place * col_count + col_place) * rows_out
    row_mask = listed_mask(block_lists, (first_row + lax.iota(jnp.int32, rows_out)) // BS)
    inverse_panel = jnp.transpose(summed, (1, 0, 2)) * row_mask[:, :, None]
    arrived = lax.all_to_all(inverse_panel, "col", split_axis=2, concat_axis=1, tiled=True)
    inverse_rows = jnp.transpose(arrived, (0, 2, 1))
    return (inverse_panel, inverse_rows)


def solution(mesh):
    in_specs = (P("row", "col"), P(None, "row", "col"), P())
    out_specs = (P(None, ("row", "col"), None), P(None, "col", "row"))
    return jax.shard_map(
        per_device, mesh=mesh, in_specs=in_specs, out_specs=out_specs, check_vma=False
    )
```

profile of v0, /device:TPU:1, one launch (start us, length us, event | category | flops | bytes accessed | tf_op | source)
XLA Modules:
  0.0 525.2 jit_solution(5785872457603567026)
XLA Ops:
  7.2 0.0 copy-start
  7.2 0.0 all-gather.2.cloned.1.call-start
  7.2 0.9 compare_reduce_fusion
  8.2 1.5 broadcast_multiply_fusion
  9.7 0.0 all-gather.2.cloned.1.call-update
  9.7 0.0 all-reduce.3.cloned.1.call-start
  9.8 81.8 %all-gather.2.cloned.1.call-done = f32[2,256,640]{2,1,0:T(8,128)} async-done(((f32[2,16,640]{2,1,0:T(8,128)}), f32[2,256,640]{2,1,0:T(8,128)}) %all-gather.2.cloned.1.call-update) | async-done | bytes 1310736 | tf_op jit(solution)/shard_map/all_gather | solution.py:21
  91.6 0.0 copy-done
  91.6 9.2 %fusion.5 = f32[1280,2,256]{0,2,1:T(8,128)} fusion(f32[2,256,640]{2,1,0:T(8,128)} %all-gather.2.cloned.1.call-done, f32[1280,640]{1,0:T(8,128)S(1)} %copy-done), kind=kOutput, calls=%fused_computation.3 | convolution fusion | flops 5033820160 | bytes 7208960 | tf_op jit(solution)/shard_map/ic,swc->isw/dot_general | solution.py:24
  100.9 5.2 copy.11
  106.0 0.0 copy-start.1
  106.0 0.0 all-reduce.3.cloned.1.call-update
  106.1 0.6 copy-done.1
  106.7 0.1 compare_reduce_fusion.1
  106.8 0.1 copy.12
  106.9 1.3 dynamic-slice
  108.8 370.7 %all-reduce.3.cloned.1.call-done = f32[1280,2,256]{2,1,0:T(2,128)} async-done(((f32[1280,2,256]{2,1,0:T(2,128)}), f32[1280,2,256]{2,1,0:T(2,128)}) %all-reduce.3.cloned.1.call-update) | async-done | bytes 2621456
  479.5 1.6 fusion.8
  481.2 1.0 copy.13
  482.2 1.1 reshape.37
  483.3 14.3 %all-to-all-start = ((f32[32,1,640]{2,1,0:T(1,128)}), f32[32,1,640]{2,1,0:T(1,128)S(1)}, u32[]{:S(2)}, u32[]{:S(2)}) async-start(f32[32,1,640]{2,1,0:T(1,128)} %reshape.37), calls=%async_computation | async-start | bytes 163840 | tf_op jit(solution)/shard_map/all_to_all | solution.py:38
  497.6 1.5 copy.15
  499.1 13.2 %all-to-all-done = f32[32,1,640]{2,1,0:T(1,128)S(1)} async-done(((f32[32,1,640]{2,1,0:T(1,128)}), f32[32,1,640]{2,1,0:T(1,128)S(1)}, u32[]{:S(2)}, u32[]{:S(2)}) %all-to-all-start) | async-done | bytes 81952 | tf_op jit(solution)/shard_map/all_to_all | solution.py:38
  512.4 0.6 broadcast.51
  513.0 1.5 reduce
  514.5 1.3 reshape.38
  515.8 0.8 copy.14
  516.6 1.7 all_to_all.16
  (4 shorter events, 0.0 us)
Async XLA Ops:
  7.2 84.5 %copy-start = (f32[1280,640]{1,0:T(8,128)S(1)}, f32[1280,640]{1,0:T(8,128)}, u32[]{:S(2)}) copy-start(f32[1280,640]{1,0:T(8,128)} %param.3) | copy-start | bytes 9830404
  7.2 84.5 %all-gather.2.cloned.1.call-start = ((), (), s32[]{:S(2)}) async-start(), calls=%async_computation.1 | async-start | bytes 1392640 | tf_op jit(solution)/shard_map/all_gather | solution.py:21
  9.7 469.8 %all-reduce.3.cloned.1.call-start = ((), (), s32[]{:S(2)}) async-start(), calls=%async_computation.2 | async-start | bytes 5242880
  106.0 0.7 copy-start.1
  483.3 29.1 %all-to-all-start = ((f32[32,1,640]{2,1,0:T(1,128)}), f32[32,1,640]{2,1,0:T(1,128)S(1)}, u32[]{:S(2)}, u32[]{:S(2)}) async-start(f32[32,1,640]{2,1,0:T(1,128)} %reshape.37), calls=%async_computation | async-start | bytes 163840 | tf_op jit(solution)/shard_map/all_to_all | solution.py:38
Sparse Core Ops, SparseCore 0:
  10.6 80.9 all-gather.1
  106.2 373.3 all-reduce.2
where the time goes:
time: 526 us; the launch traced here: 525 us
  waiting for transfers between devices  466 us (89%)
  local copies, waits for them, and re-layouts  15.2 us (3%)
  between operations  14.8 us (3%)
  starting transfers between devices  14.4 us (3%)
  matrix products  9.24 us (2%)
  other arithmetic  5.73 us (1%)
    unnamed x3, waiting for transfers between devices  371 us
    all_gather x1, waiting for transfers between devices, per_device(): gathered = lax.all_gather(masked, 'row', axis=1, tiled=True)  81.8 us
    all_to_all x1, starting transfers between devices, per_device(): lax.all_to_all(inverse_panel, 'col', split_axis=2, concat_axis=1, tiled=T...  14.3 us
    all_to_all x1, waiting for transfers between devices, per_device(): lax.all_to_all(inverse_panel, 'col', split_axis=2, concat_axis=1, tiled=T...  13.2 us
  transfers between devices with their start and end apart: 3, of which 3 were waited for; matrix products, arithmetic and copies ran while one was open for 1% of the time, Pallas kernels for 0%

commit v1 on v0

--- a/solution.py
+++ b/solution.py
@@ -18,7 +18,9 @@
     col_place = lax.axis_index("col")
     col_blocks = (col_place * local_cols + lax.iota(jnp.int32, local_cols)) // BS
     masked = factor_rows * listed_mask(block_lists, col_blocks)[:, None, :]
-    gathered = lax.all_gather(masked, "row", axis=1, tiled=True)
+    gathered = jnp.concatenate(
+        lax.all_to_all(jnp.stack([masked] * lax.axis_size("row")), "row", 0, 0), axis=1
+    )
     rows_out = local_rows // col_count
     summed = lax.psum_scatter(
         -jnp.einsum(

time: 526 us -> 475 us (0.903)
  waiting for transfers between devices: 466 us -> 376 us
  blocking collectives: 0 us -> 40.5 us
    all_gather x1 -> x0, waiting for transfers between devices: 81.8 us -> none  [per_device(): gathered = lax.all_gather(masked, 'row', axis=1, tiled=True)]
    all_to_all x0 -> x1, blocking collectives: none -> 40.5 us  [per_device(): lax.all_to_all(jnp.stack([masked] * lax.axis_size('row')), 'row', 0, 0)]
    unnamed x3 -> x2, waiting for transfers between devices: 371 us -> 363 us
  transfers between devices with their start and end apart: 3 -> 2, of which waited for: 3 -> 2; matrix products, arithmetic and copies ran while one was open for 1% -> 1% of each run, Pallas kernels for 0% -> 0%
where the time goes in v1:
time: 475 us; the launch traced here: 474 us
  waiting for transfers between devices  376 us (79%)
  blocking collectives  40.5 us (9%)
  local copies, waits for them, and re-layouts  15.4 us (3%)
  between operations  14.8 us (3%)
  starting transfers between devices  14.3 us (3%)
  matrix products  7.96 us (2%)
  other arithmetic  5.1 us (1%)
    unnamed x2, waiting for transfers between devices  363 us
    all_to_all x1, blocking collectives, per_device(): lax.all_to_all(jnp.stack([masked] * lax.axis_size('row')), 'row', 0, 0)  40.5 us
    all_to_all x1, starting transfers between devices, per_device(): lax.all_to_all(inverse_panel, 'col', split_axis=2, concat_axis=1, tiled=T...  14.3 us
    all_to_all x1, waiting for transfers between devices, per_device(): lax.all_to_all(inverse_panel, 'col', split_axis=2, concat_axis=1, tiled=T...  13.2 us
  transfers between devices with their start and end apart: 2, of which 2 were waited for; matrix products, arithmetic and copies ran while one was open for 1% of the time, Pallas kernels for 0%

profile of v1, /device:TPU:1, one launch (start us, length us, event | category | flops | bytes accessed | tf_op | source)
XLA Modules:
  0.0 474.1 jit_solution(17659881285091021186)
XLA Ops:
  7.2 0.0 copy-start
  7.2 0.0 all-reduce.3.cloned.1.call-start
  7.2 0.9 compare_reduce_fusion
  8.2 0.9 broadcast_multiply_fusion
  9.1 0.1 stack.2
  9.2 40.5 %all_to_all.23 = f32[16,2,16,640]{3,2,1,0:T(8,128)S(1)} all-to-all(f32[16,2,16,640]{3,2,1,0:T(8,128)S(1)} %stack.2), channel_id=1, replica_groups=mesh['row'=16,'col'=32] {'row'}, dimensions={0} | all-to-all | bytes 2621440 | tf_op jit(solution)/shard_map/all_to_all | solution.py:22
  49.7 0.1 copy.12
  49.8 0.0 copy-done
  49.9 8.0 %fusion.5 = f32[1280,2,256]{0,2,1:T(8,128)} fusion(f32[2,256,640]{2,1,0:T(8,128)S(1)} %bitcast.27, f32[1280,640]{1,0:T(8,128)S(1)} %copy-done), kind=kOutput, calls=%fused_computation.3 | convolution fusion | flops 5033820160 | bytes 7208960 | tf_op jit(solution)/shard_map/ic,swc->isw/dot_general | solution.py:26
  57.8 5.1 %copy.13 = f32[1280,2,256]{2,1,0:T(2,128)} copy(f32[1280,2,256]{0,2,1:T(8,128)} %fusion.5) | data formatting | bytes 5242880 | tf_op jit(solution)/shard_map/neg | solution.py:26
  63.0 0.0 copy-start.1
  63.0 0.0 all-reduce.3.cloned.1.call-update
  63.0 0.6 copy-done.1
  63.6 0.1 compare_reduce_fusion.1
  63.7 0.1 copy.14
  63.8 1.3 dynamic-slice
  65.7 362.7 %all-reduce.3.cloned.1.call-done = f32[1280,2,256]{2,1,0:T(2,128)} async-done(((f32[1280,2,256]{2,1,0:T(2,128)}), f32[1280,2,256]{2,1,0:T(2,128)}) %all-reduce.3.cloned.1.call-update) | async-done | bytes 2621456
  428.5 1.6 fusion.8
  430.1 1.0 copy.15
  431.1 1.1 reshape.47
  432.2 14.3 %all-to-all-start.1 = ((f32[32,1,640]{2,1,0:T(1,128)}), f32[32,1,640]{2,1,0:T(1,128)S(1)}, u32[]{:S(2)}, u32[]{:S(2)}) async-start(f32[32,1,640]{2,1,0:T(1,128)} %reshape.47), calls=%async_computation.1 | async-start | bytes 163840 | tf_op jit(solution)/shard_map/all_to_all | solution.py:40
  446.5 1.5 copy.17
  448.1 13.2 %all-to-all-done.1 = f32[32,1,640]{2,1,0:T(1,128)S(1)} async-done(((f32[32,1,640]{2,1,0:T(1,128)}), f32[32,1,640]{2,1,0:T(1,128)S(1)}, u32[]{:S(2)}, u32[]{:S(2)}) %all-to-all-start.1) | async-done | bytes 81952 | tf_op jit(solution)/shard_map/all_to_all | solution.py:40
  461.3 0.6 broadcast.53
  461.9 1.5 reduce
  463.4 1.3 reshape.48
  464.7 0.8 copy.16
  465.5 1.7 all_to_all.20
  (4 shorter events, 0.0 us)
Async XLA Ops:
  7.2 42.7 %copy-start = (f32[1280,640]{1,0:T(8,128)S(1)}, f32[1280,640]{1,0:T(8,128)}, u32[]{:S(2)}) copy-start(f32[1280,640]{1,0:T(8,128)} %param.3) | copy-start | bytes 9830404
  7.2 421.3 %all-reduce.3.cloned.1.call-start = ((), (), s32[]{:S(2)}) async-start(), calls=%async_computation.2 | async-start | bytes 5242880
  63.0 0.7 copy-start.1
  432.2 29.1 %all-to-all-start.1 = ((f32[32,1,640]{2,1,0:T(1,128)}), f32[32,1,640]{2,1,0:T(1,128)S(1)}, u32[]{:S(2)}, u32[]{:S(2)}) async-start(f32[32,1,640]{2,1,0:T(1,128)} %reshape.47), calls=%async_computation.1 | async-start | bytes 163840 | tf_op jit(solution)/shard_map/all_to_all | solution.py:40
Sparse Core Ops, SparseCore 0:
  63.1 365.3 all-reduce.2
